TPU v7x, 32 devices: a whole 2x2x4 slice. The times are simulated.
32 devices in a mesh: seq: 8 (over z, x), head: 4 (over y, core).
Axes of the slice: x: 2, y: 2, z: 4, core: 2. Of those that a mesh axis runs over, the one named last changes fastest.
Arguments:
- teacher_query: bfloat16 [2, 2048, 8192], P(None, ('seq', 'head')), may hold values from -6 to 6
- student_query: bfloat16 [2, 2048, 8192], P(None, ('seq', 'head')), may hold values from -6 to 6
- kept_heads: int32 [40], replicated, may hold values from 0 to 63, as said below
Outputs:
- relation_loss: float32 [2, 64, 2048], P(None, 'head', 'seq')
Inputs may be any that keep to these rules, and one draw needn't show every extreme that they name: `kept_heads`: the 40 entries are distinct, and 0 and 63 are among them.
All inputs are finite; a program needn't handle non-finite values.
Results may differ from a plain program's by a relative error of at most 0.0003.
Values may be sent and summed in bfloat16 or wider, within the bound.
No kernel may reach another device: no remote copies, remote signals or barrier semaphores. Data moves between devices by JAX's collectives and lax.ppermute only.
A program may use at most 128 MiB of HBM per device.

v0:
```python
import jax
import jax.numpy as jnp
from jax import lax
from jax.sharding import PartitionSpec as P

HEADS = 64
HD = 128
KEPT = 40
RELH = 64
TREL = 128
SREL = 80


NEG_FILL = -1e30


def fresh_stats(head_count, query_count):
    lowest = jnp.full((head_count, query_count), NEG_FILL, jnp.float32)
    zeros_block = jnp.zeros((head_count, query_count), jnp.float32)
    return (lowest, zeros_block, zeros_block, lowest, zeros_block)


def relation_update(running, query_pair, key_pair, query_pos, key_pos, scales):
    top_t, total_t, cross_sum, top_s, total_s = running
    teach_scores = (
        jnp.einsum("qhd,khd->hqk", query_pair[0], key_pair[0], preferred_element_type=jnp.float32)
        * scales[0]
    )
    stud_scores = (
        jnp.einsum("qhd,khd->hqk", query_pair[1], key_pair[1], preferred_element_type=jnp.float32)
        * scales[1]
    )
    allowed = key_pos[None, :] <= query_pos[:, None]
    teach_scores = jnp.where(allowed[None], teach_scores, NEG_FILL)
    stud_scores = jnp.where(allowed[None], stud_scores, NEG_FILL)
    new_top_t = jnp.maximum(top_t, jnp.max(teach_scores, axis=2))
    new_top_s = jnp.maximum(top_s, jnp.max(stud_scores, axis=2))
    weights_t = jnp.exp(teach_scores - new_top_t[:, :, None])
    weights_s = jnp.exp(stud_scores - new_top_s[:, :, None])
    decay_t = jnp.exp(top_t - new_top_t)
    decay_s = jnp.exp(top_s - new_top_s)
    total_t = total_t * decay_t + jnp.sum(weights_t, axis=2)
    cross_sum = cross_sum * decay_t + jnp.sum(weights_t * (teach_scores - stud_scores), axis=2)
    total_s = total_s * decay_s + jnp.sum(weights_s, axis=2)
    return (new_top_t, total_t, cross_sum, new_top_s, total_s)


def finish_rows(running):
    top_t, total_t, cross_sum, top_s, total_s = running
    return cross_sum / total_t - top_t - jnp.log(total_t) + top_s + jnp.log(total_s)


def fold_keys(running, query_pair, query_pos, key_pair, last_query, scales):
    key_length = key_pair[0].shape[0]
    key_block = 512
    steps_total = key_length // key_block

    def one_block(block_number, current):
        row_start = block_number * key_block
        block_t = lax.dynamic_slice_in_dim(key_pair[0], row_start, key_block, 0)
        block_s = lax.dynamic_slice_in_dim(key_pair[1], row_start, key_block, 0)
        key_pos = row_start + jnp.arange(key_block, dtype=jnp.int32)
        return relation_update(current, query_pair, (block_t, block_s), query_pos, key_pos, scales)

    needed = jnp.clip(last_query // key_block + 1, 0, steps_total)
    return lax.fori_loop(0, needed, one_block, running)


def batch_inside(local, head_count, width):
    seq_count_b, rows, columns = local.shape
    folded = local.reshape(seq_count_b, rows, head_count, width)
    return jnp.transpose(folded, (1, 0, 2, 3)).reshape(rows, seq_count_b * head_count * width)


def shards(teacher_query, student_query, kept_heads):
    batch_count = student_query.shape[0]
    token_rows = student_query.shape[1]
    split_heads = student_query.reshape(batch_count, token_rows, HEADS, HD)
    picked = jnp.take(split_heads, kept_heads, axis=2).reshape(batch_count, token_rows, KEPT * HD)
    teach_local, stud_local = (
        lax.all_to_all(teacher_query, "head", split_axis=2, concat_axis=1, tiled=True),
        lax.all_to_all(picked, "head", split_axis=2, concat_axis=1, tiled=True),
    )
    local_rows = teach_local.shape[1]
    head_count = RELH // lax.axis_size("head")
    wide_heads = batch_count * head_count
    teach_flat = batch_inside(teach_local, head_count, TREL)
    stud_flat = batch_inside(stud_local, head_count, SREL)
    position = lax.axis_index("seq")
    scales = (TREL ** (-0.5), SREL ** (-0.5))
    teach_heads = teach_flat.reshape(local_rows, wide_heads, TREL)
    stud_heads = stud_flat.reshape(local_rows, wide_heads, SREL)
    query_pos = position * local_rows + jnp.arange(local_rows, dtype=jnp.int32)
    last_query = position * local_rows + local_rows - 1
    key_pair = (
        lax.all_gather(teach_flat, "seq", axis=0, tiled=True).reshape(-1, wide_heads, TREL),
        lax.all_gather(stud_flat, "seq", axis=0, tiled=True).reshape(-1, wide_heads, SREL),
    )
    running = fold_keys(
        fresh_stats(wide_heads, local_rows),
        (teach_heads, stud_heads),
        query_pos,
        key_pair,
        last_query,
        scales,
    )
    return finish_rows(running).reshape(batch_count, head_count, local_rows)


def solution(mesh):
    placed = (P(None, ("seq", "head"), None), P(None, ("seq", "head"), None), P())
    return jax.shard_map(
        shards, mesh=mesh, in_specs=placed, out_specs=P(None, "head", "seq"), check_vma=False
    )
```

profile of v0, /device:TPU:25, one launch (start us, length us, event | category | flops | bytes accessed | tf_op | source)
XLA Modules:
  0.0 599.8 jit_solution(4044456868605462397)
XLA Ops:
  12.8 4.1 copy.24
  16.9 3.8 reshape.85
  20.6 19.5 %all_to_all.30 = bf16[4,2,81920]{2,1,0:T(2,128)(2,1)S(1)} all-to-all(bf16[4,2,81920]{2,1,0:T(2,128)(2,1)S(1)} %reshape.85), channel_id=1, replica_groups=mesh['seq'=8,'head'=4] {'head'}, dimensions={0} | all-to-all | bytes 2621440 | tf_op jit(solution)/shard_map/all_to_all | solution.py:82
  43.1 6.3 %copy.31 = bf16[2,64,4,1280]{3,2,1,0:T(4,128)(2,1)S(1)} copy(bf16[2,64,4,1280]{1,0,3,2:T(2,128)(2,1)} %bitcast.75) | data formatting | bytes 2621440 | tf_op jit(solution)/shard_map/all_to_all | solution.py:82
  55.5 9.5 %copy.18 = bf16[2,64,8192]{1,0,2:T(2,128)(2,1)} copy(bf16[2,64,8192]{2,1,0:T(8,128)(2,1)} %param.5) | data formatting | bytes 4194304 | tf_op args[0]
  65.0 5.1 reshape.83
  70.1 29.1 %all_to_all.31 = bf16[4,2,131072]{2,1,0:T(2,128)(2,1)} all-to-all(bf16[4,2,131072]{2,1,0:T(2,128)(2,1)S(1)} %reshape.83), channel_id=1, replica_groups=mesh['seq'=8,'head'=4] {'head'}, dimensions={0} | all-to-all | bytes 4194304 | tf_op jit(solution)/shard_map/all_to_all | solution.py:81
  99.2 5.8 reshape.84
  105.1 9.1 %copy.19 = bf16[2,64,4,2048]{3,1,2,0:T(8,128)(2,1)S(1)} copy(bf16[2,64,4,2048]{1,0,3,2:T(2,128)(2,1)} %bitcast.71) | data formatting | bytes 4194304 | tf_op jit(solution)/shard_map/all_to_all | solution.py:81
  119.2 85.5 %all-gather.5.cloned.1.call-done = bf16[2048,2560]{0,1:T(8,128)(2,1)} async-done(((bf16[256,2560]{0,1:T(8,128)(2,1)}), bf16[2048,2560]{0,1:T(8,128)(2,1)}) %all-gather.5.cloned.1.call-update) | async-done | bytes 10485776 | tf_op jit(solution)/shard_map/all_gather | solution.py:97
  204.7 227.6 %all-gather.3.cloned.1.call-done = bf16[2048,4096]{0,1:T(8,128)(2,1)} async-done(((bf16[256,4096]{0,1:T(8,128)(2,1)}), bf16[2048,4096]{0,1:T(8,128)(2,1)}) %all-gather.3.cloned.1.call-update) | async-done | bytes 16777232 | tf_op jit(solution)/shard_map/all_gather | solution.py:96
  432.9 158.5 %while.19 = (s32[]{:T(128)}, f32[32,256]{1,0:T(8,128)S(1)}, f32[32,256]{1,0:T(8,128)}, f32[32,256]{1,0:T(8,128)S(1)}, f32[32,256]{1,0:T(8,128)S(1)}, /*index=5*/...) while((s32[]{:T(128)}, f32[32,256]{1,0:T(8,128)S(1)}, ...), condition=%wide.region_6.7_spmd.clone, body=%wide.region_0.6_spmd.clone.sunk | while | flops 1816306432 | bytes 95754512 | solution.py:66
  433.0 10.3 %fusion.23 = f32[32,512,256]{2,1,0:T(8,128)} fusion(bf16[256,32,128]{2,0,1:T(8,128)(2,1)S(1)} %get-tuple-element.306, bf16[2048,32,128]{0,2,1:T(8,128)(2,1)} %get-tuple-element.305, s32[]{:T(128)S(6)} %select_n.57), kind=kOutput, calls=%fused_computation.10.clone.1 | convolution fusion | flops 1073741824 | bytes 23068676 | tf_op jit(solution)/shard_map/while/body/qhd,khd->hqk/dot_general | solution.py:26
  443.3 14.0 %fusion.24 = (f32[32,256]{1,0:T(8,128)S(1)}, f32[32,256]{1,0:T(8,128)S(1)}, f32[32,512,256]{2,1,0:T(8,128)}) fusion(pred[256,512]{0,1:T(8,128)(4,1)S(1)} %broadcast_compare_fusion.2, f32[32,512,256]{2,1,0:T(8,128)} %fusion.23, bf16[256,32,80]{0,2,1:T(8,128)(2,1)S(1)} %get-tuple-element.308, bf16[2048,32,80]{0,2,1:T(8,128)(2,1)} %get-tuple-element.307, ...), kind=kOutput, calls=%fused_computation.9.clone.1 | convolution fusion | flops 696238080 | bytes 37683204 | tf_op jit(solution)/shard_map/while/body/qhd,khd->hqk/dot_general | solution.py:30
  457.4 14.5 %multiply_reduce_fusion.2 = (f32[32,256]{1,0:T(8,128)S(1)}, f32[32,256]{1,0:T(8,128)S(1)}, f32[32,256]{1,0:T(8,128)S(1)}) fusion(f32[32,512,256]{2,1,0:T(8,128)} %fusion.23, f32[32,512,256]{2,1,0:T(8,128)} %get-tuple-element.258, f32[32,256]{1,0:T(8,128)S(1)} %max.15, pred[256,512]{0,1:T(8,128)(4,1)S(1)} %broadcast_compare_fusion.2, f32[32,256]{1,0:T(8,128)S(1)} %max.16), kind=kLoop, calls=%fused_computation.5.clone.1 | loop fusion | flops 46112768 | bytes 33849344 | tf_op jit(solution)/shard_map/while/body/reduce_sum | solution.py:43
  472.6 10.3 %fusion.23 = f32[32,512,256]{2,1,0:T(8,128)} fusion(bf16[256,32,128]{2,0,1:T(8,128)(2,1)S(1)} %get-tuple-element.306, bf16[2048,32,128]{0,2,1:T(8,128)(2,1)} %get-tuple-element.305, s32[]{:T(128)S(6)} %select_n.57), kind=kOutput, calls=%fused_computation.10.clone.1 | convolution fusion | flops 1073741824 | bytes 23068676 | tf_op jit(solution)/shard_map/while/body/qhd,khd->hqk/dot_general | solution.py:26
  482.9 14.0 %fusion.24 = (f32[32,256]{1,0:T(8,128)S(1)}, f32[32,256]{1,0:T(8,128)S(1)}, f32[32,512,256]{2,1,0:T(8,128)}) fusion(pred[256,512]{0,1:T(8,128)(4,1)S(1)} %broadcast_compare_fusion.2, f32[32,512,256]{2,1,0:T(8,128)} %fusion.23, bf16[256,32,80]{0,2,1:T(8,128)(2,1)S(1)} %get-tuple-element.308, bf16[2048,32,80]{0,2,1:T(8,128)(2,1)} %get-tuple-element.307, ...), kind=kOutput, calls=%fused_computation.9.clone.1 | convolution fusion | flops 696238080 | bytes 37683204 | tf_op jit(solution)/shard_map/while/body/qhd,khd->hqk/dot_general | solution.py:30
  497.0 14.5 %multiply_reduce_fusion.2 = (f32[32,256]{1,0:T(8,128)S(1)}, f32[32,256]{1,0:T(8,128)S(1)}, f32[32,256]{1,0:T(8,128)S(1)}) fusion(f32[32,512,256]{2,1,0:T(8,128)} %fusion.23, f32[32,512,256]{2,1,0:T(8,128)} %get-tuple-element.258, f32[32,256]{1,0:T(8,128)S(1)} %max.15, pred[256,512]{0,1:T(8,128)(4,1)S(1)} %broadcast_compare_fusion.2, f32[32,256]{1,0:T(8,128)S(1)} %max.16), kind=kLoop, calls=%fused_computation.5.clone.1 | loop fusion | flops 46112768 | bytes 33849344 | tf_op jit(solution)/shard_map/while/body/reduce_sum | solution.py:43
  512.3 10.3 %fusion.23 = f32[32,512,256]{2,1,0:T(8,128)} fusion(bf16[256,32,128]{2,0,1:T(8,128)(2,1)S(1)} %get-tuple-element.306, bf16[2048,32,128]{0,2,1:T(8,128)(2,1)} %get-tuple-element.305, s32[]{:T(128)S(6)} %select_n.57), kind=kOutput, calls=%fused_computation.10.clone.1 | convolution fusion | flops 1073741824 | bytes 23068676 | tf_op jit(solution)/shard_map/while/body/qhd,khd->hqk/dot_general | solution.py:26
  522.6 14.0 %fusion.24 = (f32[32,256]{1,0:T(8,128)S(1)}, f32[32,256]{1,0:T(8,128)S(1)}, f32[32,512,256]{2,1,0:T(8,128)}) fusion(pred[256,512]{0,1:T(8,128)(4,1)S(1)} %broadcast_compare_fusion.2, f32[32,512,256]{2,1,0:T(8,128)} %fusion.23, bf16[256,32,80]{0,2,1:T(8,128)(2,1)S(1)} %get-tuple-element.308, bf16[2048,32,80]{0,2,1:T(8,128)(2,1)} %get-tuple-element.307, ...), kind=kOutput, calls=%fused_computation.9.clone.1 | convolution fusion | flops 696238080 | bytes 37683204 | tf_op jit(solution)/shard_map/while/body/qhd,khd->hqk/dot_general | solution.py:30
  536.6 14.5 %multiply_reduce_fusion.2 = (f32[32,256]{1,0:T(8,128)S(1)}, f32[32,256]{1,0:T(8,128)S(1)}, f32[32,256]{1,0:T(8,128)S(1)}) fusion(f32[32,512,256]{2,1,0:T(8,128)} %fusion.23, f32[32,512,256]{2,1,0:T(8,128)} %get-tuple-element.258, f32[32,256]{1,0:T(8,128)S(1)} %max.15, pred[256,512]{0,1:T(8,128)(4,1)S(1)} %broadcast_compare_fusion.2, f32[32,256]{1,0:T(8,128)S(1)} %max.16), kind=kLoop, calls=%fused_computation.5.clone.1 | loop fusion | flops 46112768 | bytes 33849344 | tf_op jit(solution)/shard_map/while/body/reduce_sum | solution.py:43
  551.9 10.3 %fusion.23 = f32[32,512,256]{2,1,0:T(8,128)} fusion(bf16[256,32,128]{2,0,1:T(8,128)(2,1)S(1)} %get-tuple-element.306, bf16[2048,32,128]{0,2,1:T(8,128)(2,1)} %get-tuple-element.305, s32[]{:T(128)S(6)} %select_n.57), kind=kOutput, calls=%fused_computation.10.clone.1 | convolution fusion | flops 1073741824 | bytes 23068676 | tf_op jit(solution)/shard_map/while/body/qhd,khd->hqk/dot_general | solution.py:26
  562.2 14.0 %fusion.24 = (f32[32,256]{1,0:T(8,128)S(1)}, f32[32,256]{1,0:T(8,128)S(1)}, f32[32,512,256]{2,1,0:T(8,128)}) fusion(pred[256,512]{0,1:T(8,128)(4,1)S(1)} %broadcast_compare_fusion.2, f32[32,512,256]{2,1,0:T(8,128)} %fusion.23, bf16[256,32,80]{0,2,1:T(8,128)(2,1)S(1)} %get-tuple-element.308, bf16[2048,32,80]{0,2,1:T(8,128)(2,1)} %get-tuple-element.307, ...), kind=kOutput, calls=%fused_computation.9.clone.1 | convolution fusion | flops 696238080 | bytes 37683204 | tf_op jit(solution)/shard_map/while/body/qhd,khd->hqk/dot_general | solution.py:30
  576.2 14.5 %multiply_reduce_fusion.2 = (f32[32,256]{1,0:T(8,128)S(1)}, f32[32,256]{1,0:T(8,128)S(1)}, f32[32,256]{1,0:T(8,128)S(1)}) fusion(f32[32,512,256]{2,1,0:T(8,128)} %fusion.23, f32[32,512,256]{2,1,0:T(8,128)} %get-tuple-element.258, f32[32,256]{1,0:T(8,128)S(1)} %max.15, pred[256,512]{0,1:T(8,128)(4,1)S(1)} %broadcast_compare_fusion.2, f32[32,256]{1,0:T(8,128)S(1)} %max.16), kind=kLoop, calls=%fused_computation.5.clone.1 | loop fusion | flops 46112768 | bytes 33849344 | tf_op jit(solution)/shard_map/while/body/reduce_sum | solution.py:43
  (80 shorter events, 25.6 us)
Async XLA Ops:
  6.5 1.6 copy-start
  6.5 198.1 %all-gather.5.cloned.1.call-start = ((), (), s32[]{:S(2)}) async-start(), calls=%async_computation.3 | async-start | bytes 11796480 | tf_op jit(solution)/shard_map/all_gather | solution.py:97
  55.4 376.8 %all-gather.3.cloned.1.call-start = ((), (), s32[]{:S(2)}) async-start(), calls=%async_computation.2 | async-start | bytes 18874368 | tf_op jit(solution)/shard_map/all_gather | solution.py:96
  118.3 314.5 %copy-start.2 = (bf16[256,2,16,80]{0,3,2,1:T(8,128)(2,1)S(1)}, bf16[256,2,16,80]{0,3,2,1:T(8,128)(2,1)}, u32[]{:S(2)}) copy-start(bf16[256,2,16,80]{0,3,2,1:T(8,128)(2,1)} %copy.27) | copy-start | bytes 3932164
  457.3 14.5 %copy-start.3 = (f32[32,256]{1,0:T(8,128)S(1)}, f32[32,256]{1,0:T(8,128)}, u32[]{:S(2)}) copy-start(f32[32,256]{1,0:T(8,128)} %get-tuple-element.284) | copy-start | bytes 98308 | tf_op jit(solution)/shard_map/while
  471.9 0.6 copy-start.4
  497.0 14.5 %copy-start.3 = (f32[32,256]{1,0:T(8,128)S(1)}, f32[32,256]{1,0:T(8,128)}, u32[]{:S(2)}) copy-start(f32[32,256]{1,0:T(8,128)} %get-tuple-element.284) | copy-start | bytes 98308 | tf_op jit(solution)/shard_map/while
  511.5 0.6 copy-start.4
  536.6 14.5 %copy-start.3 = (f32[32,256]{1,0:T(8,128)S(1)}, f32[32,256]{1,0:T(8,128)}, u32[]{:S(2)}) copy-start(f32[32,256]{1,0:T(8,128)} %get-tuple-element.284) | copy-start | bytes 98308 | tf_op jit(solution)/shard_map/while
  551.1 0.6 copy-start.4
  576.2 14.5 %copy-start.3 = (f32[32,256]{1,0:T(8,128)S(1)}, f32[32,256]{1,0:T(8,128)}, u32[]{:S(2)}) copy-start(f32[32,256]{1,0:T(8,128)} %get-tuple-element.284) | copy-start | bytes 98308 | tf_op jit(solution)/shard_map/while
  590.7 0.6 copy-start.4
  591.4 1.6 copy-start.1
Sparse Core Ops, SparseCore 0:
  55.5 149.0 all-gather.4
  206.7 225.4 all-gather.2
where the time goes:
time: 601 us; the launch traced here: 600 us
  waiting for transfers between devices  313 us (52%)
  matrix products  97.2 us (16%)
  local copies, waits for them, and re-layouts  65.2 us (11%)
  other arithmetic  61.9 us (10%)
  blocking collectives  48.6 us (8%)
  between operations  13.5 us (2%)
    all_gather x1, waiting for transfers between devices, shards(): lax.all_gather(teach_flat, 'seq', axis=0, tiled=True)  228 us
    all_gather x1, waiting for transfers between devices, shards(): lax.all_gather(stud_flat, 'seq', axis=0, tiled=True)  85.5 us
    reduce_sum x4, other arithmetic, relation_update(): jnp.sum(weights_t * (teach_scores - stud_scores), axis=2)  57.8 us
    dot_general x4, matrix products, relation_update(): jnp.einsum('qhd,khd->hqk', query_pair[1], key_pair[1], preferred_element_...  56 us
    dot_general x4, matrix products, relation_update(): jnp.einsum('qhd,khd->hqk', query_pair[0], key_pair[0], preferred_element_...  41.1 us
    all_to_all x1, blocking collectives, shards(): lax.all_to_all(teacher_query, 'head', split_axis=2, concat_axis=1, tiled=...  29.1 us
    unnamed x13, local copies, waits for them, and re-layouts  28.7 us
    all_to_all x1, blocking collectives, shards(): lax.all_to_all(picked, 'head', split_axis=2, concat_axis=1, tiled=True)  19.5 us
  transfers between devices with their start and end apart: 2, of which 2 were waited for; matrix products, arithmetic and copies ran while one was open for 6% of the time, Pallas kernels for 0%

commit v1 on v0

--- a/solution.py
+++ b/solution.py
@@ -1,6 +1,11 @@
+import functools
+import math
+
 import jax
 import jax.numpy as jnp
 from jax import lax
+from jax.experimental import pallas as pl
+from jax.experimental.pallas import tpu as pltpu
 from jax.sharding import PartitionSpec as P
 
 HEADS = 64
@@ -9,6 +14,191 @@
 RELH = 64
 TREL = 128
 SREL = 80
+LANES = 128
+CHUNK = 32
+GROUP = 4
+BLOCK = 256
+LOG2E = math.log2(math.e)
+LN2 = math.log(2.0)
+
+
+def pack_kernel(kept_ref, teach_ref, *refs):
+    heads, out_ref = refs[:-1], refs[-1]
+    lane = lax.broadcasted_iota(jnp.int32, (2 * HD // 2, LANES), 1)
+    small_lane = lax.broadcasted_iota(jnp.int32, (CHUNK, LANES), 1)
+    rows = out_ref.shape[3]
+    del rows
+    picked = [head[...].reshape(LANES, LANES) for head in heads]
+    for i in range(GROUP):
+        for w in range(2):
+            start = (2 * i + w) * TREL
+            out_ref[0, i, 0, w * LANES : (w + 1) * LANES, :] = teach_ref[:, :, start : start + TREL].reshape(
+                LANES, LANES
+            )
+        first, last = picked[i], picked[i + 1]
+        main = first if i == 0 else jnp.where(lane >= CHUNK * i, first, last)
+        out_ref[0, i, 0, 2 * LANES : 3 * LANES, :] = main
+        extra = jnp.zeros((CHUNK, LANES), jnp.float32)
+        for g in range(4):
+            part = last[g * CHUNK : (g + 1) * CHUNK].astype(jnp.float32)
+            if g:
+                part = pltpu.roll(part, g * CHUNK, 1)
+            extra = jnp.where(small_lane // CHUNK == (i + g) % 4, part, extra)
+        out_ref[0, i, 0, 3 * LANES :, :] = extra.astype(jnp.bfloat16)
+
+
+def pack(teacher, student, kept, seq_size, head_size):
+    batch, rows, _ = teacher.shape
+    message = 3 * LANES + CHUNK
+    groups = RELH // (2 * GROUP)
+
+    def out_map(g, kept_ref):
+        first = g * GROUP
+        return ((first % seq_size) // GROUP, 0, first // seq_size, 0, 0)
+
+    def head_map(m, g, kept_ref):
+        return (0, 0, kept_ref[5 * g + m])
+
+    packed = pl.pallas_call(
+        pack_kernel,
+        out_shape=jax.ShapeDtypeStruct((seq_size // GROUP, GROUP, head_size, message, LANES), jnp.bfloat16),
+        grid_spec=pltpu.PrefetchScalarGridSpec(
+            num_scalar_prefetch=1,
+            grid=(groups,),
+            in_specs=[pl.BlockSpec((batch, rows, 2 * GROUP * TREL), lambda g, kept_ref: (0, 0, g))]
+            + [pl.BlockSpec((batch, rows, HD), functools.partial(head_map, m)) for m in range(5)],
+            out_specs=pl.BlockSpec((1, GROUP, 1, message, LANES), out_map),
+        ),
+        name="pack_messages",
+    )(kept, teacher, *([student] * 5))
+    return packed.reshape(seq_size * head_size, message, LANES)
+
+
+def nt_dot(a, b):
+    return lax.dot_general(a, b, (((1,), (1,)), ((), ())), preferred_element_type=jnp.float32)
+
+
+def relation_kernel(slot_ref, got_ref, out_ref, teach, stud, shift_t, shift_s, acc_t, acc_c, acc_s):
+    peers = got_ref.shape[0]
+    half = LANES // 2
+    count = peers * half
+    units = teach.shape[0]
+    scale_t = TREL ** (-0.5) * LOG2E
+    scale_s = SREL ** (-0.5) * LOG2E
+    lane = lax.broadcasted_iota(jnp.int32, (half, LANES), 1)
+    rel = (lane - CHUNK * slot_ref[0]) & (LANES - 1)
+    in_first = rel < SREL
+    in_tail = rel < CHUNK
+    zero = jnp.zeros((half, LANES), jnp.float32)
+
+    def unpack(j, carry):
+        at = pl.ds(pl.multiple_of(j * half, half), half)
+        tail = got_ref[j, 3 * LANES :, :].astype(jnp.float32)
+        for b in range(2):
+            for w in range(2):
+                teach[2 * b + w, at, :] = got_ref[j, w * LANES + b * half : w * LANES + (b + 1) * half, :]
+            main = got_ref[j, 2 * LANES + b * half : 2 * LANES + (b + 1) * half, :].astype(jnp.float32)
+            parts = [
+                pltpu.roll(tail, (LANES - g * CHUNK) % LANES, 1) if g else tail for g in (2 * b, 2 * b + 1)
+            ]
+            own = jnp.concatenate(parts, axis=0)
+            stud[2 * b, at, :] = jnp.where(in_first, main, zero).astype(jnp.bfloat16)
+            stud[2 * b + 1, at, :] = jnp.where(in_tail, own, jnp.where(in_first, zero, main)).astype(jnp.bfloat16)
+        return carry
+
+    lax.fori_loop(0, peers, unpack, 0)
+
+    ones = jnp.ones((8, LANES), jnp.bfloat16)
+
+    def shifts(ref, u, scale):
+        rows = ref[u]
+        square = nt_dot(ones, rows * rows)
+        norm = jnp.sqrt(square)
+        top = jnp.max(norm, axis=1, keepdims=True)
+        return norm * (norm + top) * (0.5 * scale)
+
+    key_in = lax.broadcasted_iota(jnp.int32, (BLOCK // 8, 8, BLOCK), 0) * 8 + lax.broadcasted_iota(
+        jnp.int32, (BLOCK // 8, 8, BLOCK), 1
+    )
+    query_in = lax.broadcasted_iota(jnp.int32, (BLOCK // 8, 8, BLOCK), 2)
+    allowed = key_in <= query_in
+
+    def unit(u, carry):
+        shift_t[...] = shifts(teach, u, scale_t)
+        shift_s[...] = shifts(stud, u, scale_s)
+        for q in range(count // BLOCK):
+            cols = slice(q * BLOCK, (q + 1) * BLOCK)
+            query_t = teach[u, cols, :]
+            query_s = stud[u, cols, :]
+            off_t = shift_t[:, cols]
+            off_s = shift_s[:, cols]
+            sum_t = jnp.zeros((8, BLOCK), jnp.float32)
+            sum_c = jnp.zeros((8, BLOCK), jnp.float32)
+            sum_s = jnp.zeros((8, BLOCK), jnp.float32)
+            for k in range(q + 1):
+                keys = slice(k * BLOCK, (k + 1) * BLOCK)
+                x_t = nt_dot(teach[u, keys, :], query_t).reshape(BLOCK // 8, 8, BLOCK) * scale_t - off_t[None]
+                x_s = nt_dot(stud[u, keys, :], query_s).reshape(BLOCK // 8, 8, BLOCK) * scale_s - off_s[None]
+                w_t = jnp.exp2(x_t)
+                w_s = jnp.exp2(x_s)
+                if k == q:
+                    w_t = jnp.where(allowed, w_t, 0.0)
+                    w_s = jnp.where(allowed, w_s, 0.0)
+                sum_t += jnp.sum(w_t, axis=0)
+                sum_c += jnp.sum(w_t * (x_t - x_s), axis=0)
+                sum_s += jnp.sum(w_s, axis=0)
+            acc_t[u, q] = sum_t
+            acc_c[u, q] = sum_c
+            acc_s[u, q] = sum_s
+        return carry
+
+    lax.fori_loop(0, units, unit, 0)
+    for u in range(units):
+        total_t = jnp.sum(acc_t[u], axis=1)
+        total_c = jnp.sum(acc_c[u], axis=1)
+        total_s = jnp.sum(acc_s[u], axis=1)
+        out_ref[:, u, :] = (total_c / total_t - jnp.log2(total_t) + jnp.log2(total_s)) * LN2
+
+
+def relation(got, slot):
+    peers, message, _ = got.shape
+    count = peers * LANES // 2
+    blocks = count // BLOCK
+    units = 4
+    return pl.pallas_call(
+        relation_kernel,
+        out_shape=jax.ShapeDtypeStruct((blocks, units, BLOCK), jnp.float32),
+        grid_spec=pltpu.PrefetchScalarGridSpec(
+            num_scalar_prefetch=1,
+            grid=(1,),
+            in_specs=[pl.BlockSpec((peers, message, LANES), lambda i, slot_ref: (0, 0, 0), pipeline_mode=pl.Buffered(1))],
+            out_specs=pl.BlockSpec((blocks, units, BLOCK), lambda i, slot_ref: (0, 0, 0)),
+            scratch_shapes=[
+                pltpu.VMEM((units, count, LANES), jnp.bfloat16),
+                pltpu.VMEM((units, count, LANES), jnp.bfloat16),
+                pltpu.VMEM((8, count), jnp.float32),
+                pltpu.VMEM((8, count), jnp.float32),
+                pltpu.VMEM((units, blocks, 8, BLOCK), jnp.float32),
+                pltpu.VMEM((units, blocks, 8, BLOCK), jnp.float32),
+                pltpu.VMEM((units, blocks, 8, BLOCK), jnp.float32),
+            ],
+        ),
+        compiler_params=pltpu.CompilerParams(vmem_limit_bytes=48 * 1024 * 1024),
+        name="relation_loss",
+    )(slot, got)
+
+
+def packed_shards(teacher, student, kept):
+    seq_size, head_size = lax.axis_size("seq"), lax.axis_size("head")
+    batch = teacher.shape[0]
+    messages = pack(teacher, student, kept, seq_size, head_size)
+    got = lax.all_to_all(messages, ("seq", "head"), 0, 0, tiled=True)
+    slot = (lax.axis_index("seq") % GROUP).astype(jnp.int32).reshape(1)
+    mine = relation(got, slot)
+    done = lax.all_to_all(mine, "seq", 0, 0, tiled=True)
+    pair = RELH // head_size // seq_size
+    done = done.reshape(seq_size, batch, pair, BLOCK)
+    return jnp.transpose(done, (1, 0, 2, 3)).reshape(batch, RELH // head_size, BLOCK)
 
 
 NEG_FILL = -1e30
@@ -109,6 +299,25 @@
 
 def solution(mesh):
     placed = (P(None, ("seq", "head"), None), P(None, ("seq", "head"), None), P())
-    return jax.shard_map(
-        shards, mesh=mesh, in_specs=placed, out_specs=P(None, "head", "seq"), check_vma=False
-    )
+    sizes = dict(mesh.shape)
+
+    def run(teacher, student, kept):
+        seq_size, head_size = sizes["seq"], sizes["head"]
+        batch, length = teacher.shape[0], teacher.shape[1]
+        rows = length // (seq_size * head_size)
+        fits = (
+            batch * rows == LANES
+            and batch == 2
+            and seq_size % GROUP == 0
+            and RELH == 2 * seq_size * head_size
+            and length // seq_size == BLOCK
+        )
+        return jax.shard_map(
+            packed_shards if fits else shards,
+            mesh=mesh,
+            in_specs=placed,
+            out_specs=P(None, "head", "seq"),
+            check_vma=False,
+        )(teacher, student, kept)
+
+    return run

time: 601 us -> 124 us (0.21)
  the two profiles are of different devices: /device:TPU:25 before, /device:TPU:4 now
where the time goes in v1:
time: 124 us
  waiting for transfers between devices  76.5 us (62%)
  Pallas kernels  28.7 us (23%)
  blocking collectives  11.8 us (10%)
  starting transfers between devices  6.1 us (5%)
    all_to_all x1, waiting for transfers between devices, packed_shards(): got = lax.all_to_all(messages, ('seq', 'head'), 0, 0, tiled=True)  76.5 us
    pallas_call x1, Pallas kernels, relation(): pl.pallas_call(relation_kernel, out_shape=jax.ShapeDtypeStruct((blocks, u...  21.4 us
    all_to_all x1, blocking collectives, packed_shards(): done = lax.all_to_all(mine, 'seq', 0, 0, tiled=True)  11.8 us
    pallas_call x1, Pallas kernels, pack(): pl.pallas_call(pack_kernel, out_shape=jax.ShapeDtypeStruct((seq_size // G...  7.34 us
    all_to_all x1, starting transfers between devices, packed_shards(): got = lax.all_to_all(messages, ('seq', 'head'), 0, 0, tiled=True)  6.1 us
  transfers between devices with their start and end apart: 1, of which 1 were waited for; matrix products, arithmetic and copies ran while one was open for 0% of the time, Pallas kernels for 0%

profile of v1, /device:TPU:4, one launch (start us, length us, event | category | flops | bytes accessed | tf_op | source)
XLA Modules:
  0.0 123.9 jit_solution(8678810321829263504)
XLA Ops:
  0.0 7.3 %pack_messages.1 = bf16[2,4,4,416,128]{4,3,2,1,0:T(8,128)(2,1)} custom-call(s32[40]{0:T(128)} %kept_ref.1, bf16[2,64,8192]{2,1,0:T(8,128)(2,1)} %teach_ref.1, bf16[2,64,8192]{2,1,0:T(8,128)(2,1)} %refs_4_.1, bf16[2,64,8192]{2,1,0:T(8,128)(2,1)} %refs_4_.1, bf16[2,64,8192]{2,1,0:T(8,128)(2,1)} %refs_4_.1, bf16[2,64,8192]{2,1,0:T(8,128)(2,1)} %refs_4_.1, ...), custom_call_target="tpu_custom_call" | custom-call | tf_op jit(solution)/shard_map/pack_messages/pallas_call | solution.py:62
  7.3 6.1 %all-to-all-start = ((bf16[32,416,128]{2,1,0:T(8,128)(2,1)}), bf16[32,416,128]{2,1,0:T(8,128)(2,1)S(1)}, u32[]{:S(2)}, u32[]{:S(2)}) async-start(bf16[32,416,128]{2,1,0:T(8,128)(2,1)} %bitcast.3), calls=%async_computation | async-start | bytes 6815744 | tf_op jit(solution)/shard_map/all_to_all | solution.py:195
  13.5 76.5 %all-to-all-done.got_ref = bf16[32,416,128]{2,1,0:T(8,128)(2,1)S(1)} async-done(((bf16[32,416,128]{2,1,0:T(8,128)(2,1)}), bf16[32,416,128]{2,1,0:T(8,128)(2,1)S(1)}, u32[]{:S(2)}, u32[]{:S(2)}) %all-to-all-start) | async-done | bytes 3407904 | tf_op jit(solution)/shard_map/all_to_all | solution.py:195
  90.0 21.4 %relation_loss.1 = f32[8,4,256]{2,1,0:T(4,128)S(1)} custom-call(s32[1]{0:T(128)} %bitcast.slot_ref, bf16[32,416,128]{2,1,0:T(8,128)(2,1)S(1)} %all-to-all-done.got_ref), custom_call_target="tpu_custom_call" | custom-call | tf_op jit(solution)/shard_map/relation_loss/pallas_call | solution.py:168
  111.4 11.8 %all_to_all.10 = f32[8,4,256]{2,1,0:T(4,128)S(1)} all-to-all(f32[8,4,256]{2,1,0:T(4,128)S(1)} %relation_loss.1), channel_id=1, replica_groups=mesh['seq'=8,'head'=4] {'seq'}, dimensions={0} | all-to-all | bytes 65536 | tf_op jit(solution)/shard_map/all_to_all | solution.py:198
  123.2 0.6 reshape.15
  (2 shorter events, 0.0 us)
Async XLA Ops:
  7.3 82.7 %all-to-all-start = ((bf16[32,416,128]{2,1,0:T(8,128)(2,1)}), bf16[32,416,128]{2,1,0:T(8,128)(2,1)S(1)}, u32[]{:S(2)}, u32[]{:S(2)}) async-start(bf16[32,416,128]{2,1,0:T(8,128)(2,1)} %bitcast.3), calls=%async_computation | async-start | bytes 6815744 | tf_op jit(solution)/shard_map/all_to_all | solution.py:195

commit v2 on v1

--- a/solution.py
+++ b/solution.py
@@ -18,16 +18,17 @@
 CHUNK = 32
 GROUP = 4
 BLOCK = 256
+LIMIT = 6.0
 LOG2E = math.log2(math.e)
 LN2 = math.log(2.0)
+SCALE_T = TREL ** (-0.5) * LOG2E
+SCALE_S = SREL ** (-0.5) * LOG2E
 
 
 def pack_kernel(kept_ref, teach_ref, *refs):
     heads, out_ref = refs[:-1], refs[-1]
     lane = lax.broadcasted_iota(jnp.int32, (2 * HD // 2, LANES), 1)
     small_lane = lax.broadcasted_iota(jnp.int32, (CHUNK, LANES), 1)
-    rows = out_ref.shape[3]
-    del rows
     picked = [head[...].reshape(LANES, LANES) for head in heads]
     for i in range(GROUP):
         for w in range(2):
@@ -78,13 +79,40 @@
     return lax.dot_general(a, b, (((1,), (1,)), ((), ())), preferred_element_type=jnp.float32)
 
 
-def relation_kernel(slot_ref, got_ref, out_ref, teach, stud, shift_t, shift_s, acc_t, acc_c, acc_s):
+def shift_of(rows, width, factor):
+    norm = jnp.sqrt(nt_dot(jnp.ones((8, LANES), jnp.bfloat16), rows * rows))
+    return norm * (norm + LIMIT * math.sqrt(width)) * (0.5 * factor)
+
+
+def tile_sums(key_t, key_s, query_t, query_s, off_t, off_s, allowed):
+    tile = (BLOCK // 8, 8, BLOCK)
+    x_t = nt_dot(jnp.concatenate([key_t, key_t], axis=1), query_t).reshape(tile) - off_t[None]
+    x_s = nt_dot(jnp.concatenate([key_s, key_s], axis=1), query_s).reshape(tile) - off_s[None]
+    w_t = jnp.exp2(x_t)
+    w_s = jnp.exp2(x_s)
+    if allowed is not None:
+        w_t = jnp.where(allowed, w_t, 0.0)
+        w_s = jnp.where(allowed, w_s, 0.0)
+    return jnp.sum(w_t, axis=0), jnp.sum(w_t * (x_t - x_s), axis=0), jnp.sum(w_s, axis=0)
+
+
+def causal_tile():
+    tile = (BLOCK // 8, 8, BLOCK)
+    key_in = lax.broadcasted_iota(jnp.int32, tile, 0) * 8 + lax.broadcasted_iota(jnp.int32, tile, 1)
+    return key_in <= lax.broadcasted_iota(jnp.int32, tile, 2)
+
+
+def split_terms(row, scale):
+    scaled = row * scale
+    high = scaled.astype(jnp.bfloat16)
+    return high, (scaled - high.astype(jnp.float32)).astype(jnp.bfloat16)
+
+
+def relation_kernel(slot_ref, got_ref, out_ref, teach, stud, query_t, query_s, shifts, acc_t, acc_c, acc_s):
     peers = got_ref.shape[0]
     half = LANES // 2
     count = peers * half
     units = teach.shape[0]
-    scale_t = TREL ** (-0.5) * LOG2E
-    scale_s = SREL ** (-0.5) * LOG2E
     lane = lax.broadcasted_iota(jnp.int32, (half, LANES), 1)
     rel = (lane - CHUNK * slot_ref[0]) & (LANES - 1)
     in_first = rel < SREL
@@ -96,60 +124,49 @@
         tail = got_ref[j, 3 * LANES :, :].astype(jnp.float32)
         for b in range(2):
             for w in range(2):
-                teach[2 * b + w, at, :] = got_ref[j, w * LANES + b * half : w * LANES + (b + 1) * half, :]
+                key = got_ref[j, w * LANES + b * half : w * LANES + (b + 1) * half, :]
+                u = 2 * b + w
+                teach[u, at, :] = key
+                query_t[u, at, 0:LANES], query_t[u, at, LANES:] = split_terms(key.astype(jnp.float32), SCALE_T)
             main = got_ref[j, 2 * LANES + b * half : 2 * LANES + (b + 1) * half, :].astype(jnp.float32)
             parts = [
                 pltpu.roll(tail, (LANES - g * CHUNK) % LANES, 1) if g else tail for g in (2 * b, 2 * b + 1)
             ]
             own = jnp.concatenate(parts, axis=0)
-            stud[2 * b, at, :] = jnp.where(in_first, main, zero).astype(jnp.bfloat16)
-            stud[2 * b + 1, at, :] = jnp.where(in_tail, own, jnp.where(in_first, zero, main)).astype(jnp.bfloat16)
+            both = (jnp.where(in_first, main, zero), jnp.where(in_tail, own, jnp.where(in_first, zero, main)))
+            for w, row in enumerate(both):
+                u = 2 * b + w
+                stud[u, at, :] = row.astype(jnp.bfloat16)
+                query_s[u, at, 0:LANES], query_s[u, at, LANES:] = split_terms(row, SCALE_S)
         return carry
 
     lax.fori_loop(0, peers, unpack, 0)
-
-    ones = jnp.ones((8, LANES), jnp.bfloat16)
-
-    def shifts(ref, u, scale):
-        rows = ref[u]
-        square = nt_dot(ones, rows * rows)
-        norm = jnp.sqrt(square)
-        top = jnp.max(norm, axis=1, keepdims=True)
-        return norm * (norm + top) * (0.5 * scale)
-
-    key_in = lax.broadcasted_iota(jnp.int32, (BLOCK // 8, 8, BLOCK), 0) * 8 + lax.broadcasted_iota(
-        jnp.int32, (BLOCK // 8, 8, BLOCK), 1
-    )
-    query_in = lax.broadcasted_iota(jnp.int32, (BLOCK // 8, 8, BLOCK), 2)
-    allowed = key_in <= query_in
+    allowed = causal_tile()
+
+    def shift(u, carry):
+        shifts[u, 0] = shift_of(teach[u], TREL, SCALE_T)
+        shifts[u, 1] = shift_of(stud[u], SREL, SCALE_S)
+        return carry
+
+    lax.fori_loop(0, units, shift, 0)
 
     def unit(u, carry):
-        shift_t[...] = shifts(teach, u, scale_t)
-        shift_s[...] = shifts(stud, u, scale_s)
         for q in range(count // BLOCK):
             cols = slice(q * BLOCK, (q + 1) * BLOCK)
-            query_t = teach[u, cols, :]
-            query_s = stud[u, cols, :]
-            off_t = shift_t[:, cols]
-            off_s = shift_s[:, cols]
-            sum_t = jnp.zeros((8, BLOCK), jnp.float32)
-            sum_c = jnp.zeros((8, BLOCK), jnp.float32)
-            sum_s = jnp.zeros((8, BLOCK), jnp.float32)
+            sums = [jnp.zeros((8, BLOCK), jnp.float32)] * 3
             for k in range(q + 1):
                 keys = slice(k * BLOCK, (k + 1) * BLOCK)
-                x_t = nt_dot(teach[u, keys, :], query_t).reshape(BLOCK // 8, 8, BLOCK) * scale_t - off_t[None]
-                x_s = nt_dot(stud[u, keys, :], query_s).reshape(BLOCK // 8, 8, BLOCK) * scale_s - off_s[None]
-                w_t = jnp.exp2(x_t)
-                w_s = jnp.exp2(x_s)
-                if k == q:
-                    w_t = jnp.where(allowed, w_t, 0.0)
-                    w_s = jnp.where(allowed, w_s, 0.0)
-                sum_t += jnp.sum(w_t, axis=0)
-                sum_c += jnp.sum(w_t * (x_t - x_s), axis=0)
-                sum_s += jnp.sum(w_s, axis=0)
-            acc_t[u, q] = sum_t
-            acc_c[u, q] = sum_c
-            acc_s[u, q] = sum_s
+                more = tile_sums(
+                    teach[u, keys, :],
+                    stud[u, keys, :],
+                    query_t[u, cols, :],
+                    query_s[u, cols, :],
+                    shifts[u, 0, :, cols],
+                    shifts[u, 1, :, cols],
+                    allowed if k == q else None,
+                )
+                sums = [a + b for a, b in zip(sums, more)]
+            acc_t[u, q], acc_c[u, q], acc_s[u, q] = sums
         return carry
 
     lax.fori_loop(0, units, unit, 0)
@@ -176,8 +193,9 @@
             scratch_shapes=[
                 pltpu.VMEM((units, count, LANES), jnp.bfloat16),
                 pltpu.VMEM((units, count, LANES), jnp.bfloat16),
-                pltpu.VMEM((8, count), jnp.float32),
-                pltpu.VMEM((8, count), jnp.float32),
+                pltpu.VMEM((units, count, 2 * LANES), jnp.bfloat16),
+                pltpu.VMEM((units, count, 2 * LANES), jnp.bfloat16),
+                pltpu.VMEM((units, 2, 8, count), jnp.float32),
                 pltpu.VMEM((units, blocks, 8, BLOCK), jnp.float32),
                 pltpu.VMEM((units, blocks, 8, BLOCK), jnp.float32),
                 pltpu.VMEM((units, blocks, 8, BLOCK), jnp.float32),

time: 124 us -> 121 us (0.976)
  Pallas kernels: 28.7 us -> 25.7 us
    pallas_call x1, Pallas kernels: 21.4 us -> 18.4 us  [relation(): pl.pallas_call(relation_kernel, out_shape=jax.ShapeDtypeStruct((blocks, u...]
where the time goes in v2:
time: 121 us
  waiting for transfers between devices  76.5 us (63%)
  Pallas kernels  25.7 us (21%)
  blocking collectives  11.8 us (10%)
  starting transfers between devices  6.1 us (5%)
    all_to_all x1, waiting for transfers between devices, packed_shards(): got = lax.all_to_all(messages, ('seq', 'head'), 0, 0, tiled=True)  76.5 us
    pallas_call x1, Pallas kernels, relation(): pl.pallas_call(relation_kernel, out_shape=jax.ShapeDtypeStruct((blocks, u...  18.4 us
    all_to_all x1, blocking collectives, packed_shards(): done = lax.all_to_all(mine, 'seq', 0, 0, tiled=True)  11.8 us
    pallas_call x1, Pallas kernels, pack(): pl.pallas_call(pack_kernel, out_shape=jax.ShapeDtypeStruct((seq_size // G...  7.34 us
    all_to_all x1, starting transfers between devices, packed_shards(): got = lax.all_to_all(messages, ('seq', 'head'), 0, 0, tiled=True)  6.1 us
  transfers between devices with their start and end apart: 1, of which 1 were waited for; matrix products, arithmetic and copies ran while one was open for 0% of the time, Pallas kernels for 0%

profile of v2, /device:TPU:4, one launch (start us, length us, event | category | flops | bytes accessed | tf_op | source)
XLA Modules:
  0.0 120.8 jit_solution(1861514073767592614)
XLA Ops:
  0.0 7.3 %pack_messages.1 = bf16[2,4,4,416,128]{4,3,2,1,0:T(8,128)(2,1)} custom-call(s32[40]{0:T(128)} %kept_ref.1, bf16[2,64,8192]{2,1,0:T(8,128)(2,1)} %teach_ref.1, bf16[2,64,8192]{2,1,0:T(8,128)(2,1)} %refs_4_.1, bf16[2,64,8192]{2,1,0:T(8,128)(2,1)} %refs_4_.1, bf16[2,64,8192]{2,1,0:T(8,128)(2,1)} %refs_4_.1, bf16[2,64,8192]{2,1,0:T(8,128)(2,1)} %refs_4_.1, ...), custom_call_target="tpu_custom_call" | custom-call | tf_op jit(solution)/shard_map/pack_messages/pallas_call | solution.py:63
  7.3 6.1 %all-to-all-start = ((bf16[32,416,128]{2,1,0:T(8,128)(2,1)}), bf16[32,416,128]{2,1,0:T(8,128)(2,1)S(1)}, u32[]{:S(2)}, u32[]{:S(2)}) async-start(bf16[32,416,128]{2,1,0:T(8,128)(2,1)} %bitcast.3), calls=%async_computation | async-start | bytes 6815744 | tf_op jit(solution)/shard_map/all_to_all | solution.py:213
  13.5 76.5 %all-to-all-done.got_ref = bf16[32,416,128]{2,1,0:T(8,128)(2,1)S(1)} async-done(((bf16[32,416,128]{2,1,0:T(8,128)(2,1)}), bf16[32,416,128]{2,1,0:T(8,128)(2,1)S(1)}, u32[]{:S(2)}, u32[]{:S(2)}) %all-to-all-start) | async-done | bytes 3407904 | tf_op jit(solution)/shard_map/all_to_all | solution.py:213
  90.0 18.4 %relation_loss.1 = f32[8,4,256]{2,1,0:T(4,128)S(1)} custom-call(s32[1]{0:T(128)} %bitcast.slot_ref, bf16[32,416,128]{2,1,0:T(8,128)(2,1)S(1)} %all-to-all-done.got_ref), custom_call_target="tpu_custom_call" | custom-call | tf_op jit(solution)/shard_map/relation_loss/pallas_call | solution.py:185
  108.4 11.8 %all_to_all.10 = f32[8,4,256]{2,1,0:T(4,128)S(1)} all-to-all(f32[8,4,256]{2,1,0:T(4,128)S(1)} %relation_loss.1), channel_id=1, replica_groups=mesh['seq'=8,'head'=4] {'seq'}, dimensions={0} | all-to-all | bytes 65536 | tf_op jit(solution)/shard_map/all_to_all | solution.py:216
  120.2 0.6 reshape.15
  (2 shorter events, 0.0 us)
Async XLA Ops:
  7.3 82.7 %all-to-all-start = ((bf16[32,416,128]{2,1,0:T(8,128)(2,1)}), bf16[32,416,128]{2,1,0:T(8,128)(2,1)S(1)}, u32[]{:S(2)}, u32[]{:S(2)}) async-start(bf16[32,416,128]{2,1,0:T(8,128)(2,1)} %bitcast.3), calls=%async_computation | async-start | bytes 6815744 | tf_op jit(solution)/shard_map/all_to_all | solution.py:213

commit v3 on v0

--- a/solution.py
+++ b/solution.py
@@ -1,7 +1,13 @@
+import functools
+import math
+
 import jax
 import jax.numpy as jnp
 from jax import lax
+from jax.experimental import pallas as pl
+from jax.experimental.pallas import tpu as pltpu
 from jax.sharding import PartitionSpec as P
+
 
 HEADS = 64
 HD = 128
@@ -9,6 +15,321 @@
 RELH = 64
 TREL = 128
 SREL = 80
+LANES = 128
+CHUNK = 32
+GROUP = 4
+BLOCK = 256
+LIMIT = 6.0
+LOG2E = math.log2(math.e)
+LN2 = math.log(2.0)
+SCALE_T = TREL ** (-0.5) * LOG2E
+SCALE_S = SREL ** (-0.5) * LOG2E
+
+
+SEQ_SIZE = 8
+STAGES = ((0, 2), (4, 2), (2, 2), (6, 1), (7, 1))
+HEAD_SIZE = 4
+MESSAGE = 3 * LANES + CHUNK
+UNITS = 4
+ROWS = 64
+
+
+def pack_kernel(cross, kept_ref, teach_hbm, stud_hbm, *refs):
+    outs = refs[-19:-3]
+    teach, heads, sems = refs[-3:]
+    seq, head = lax.axis_index("seq"), lax.axis_index("head")
+    lane = lax.broadcasted_iota(jnp.int32, (LANES, LANES), 1)
+    small_lane = lax.broadcasted_iota(jnp.int32, (CHUNK, LANES), 1)
+    copies = []
+    for turn in range(HEAD_SIZE):
+        group = 2 * (head ^ turn) + ((seq >> 2) ^ cross)
+        width = 2 * GROUP * TREL
+        some = [
+            pltpu.make_async_copy(
+                teach_hbm.at[:, :, pl.ds(pl.multiple_of(group * width, width), width)],
+                teach.at[turn],
+                sems.at[turn, 0],
+            )
+        ]
+        for m in range(5):
+            start = pl.multiple_of(kept_ref[5 * group + m] * HD, HD)
+            some.append(
+                pltpu.make_async_copy(
+                    stud_hbm.at[:, :, pl.ds(start, HD)], heads.at[turn, m], sems.at[turn, m + 1]
+                )
+            )
+        for copy in some:
+            copy.start()
+        copies.append(some)
+    for turn in range(HEAD_SIZE):
+        for copy in copies[turn]:
+            copy.wait()
+        for step in range(GROUP):
+            i = (seq & 3) ^ step
+            out = outs[GROUP * step + turn]
+            for w in range(2):
+                start = pl.multiple_of((2 * i + w) * TREL, TREL)
+                out[w * LANES : (w + 1) * LANES, :] = teach[turn, :, :, pl.ds(start, TREL)].reshape(LANES, LANES)
+            first = heads[turn, i].reshape(LANES, LANES)
+            last = heads[turn, i + 1].reshape(LANES, LANES)
+            out[2 * LANES : 3 * LANES, :] = jnp.where(lane >= CHUNK * i, first, last)
+            extra = jnp.zeros((CHUNK, LANES), jnp.float32)
+            for g in range(4):
+                part = last[g * CHUNK : (g + 1) * CHUNK].astype(jnp.float32)
+                if g:
+                    part = pltpu.roll(part, g * CHUNK, 1)
+                extra = jnp.where(small_lane // CHUNK == ((i + g) & 3), part, extra)
+            out[3 * LANES :, :] = extra.astype(jnp.bfloat16)
+
+
+def pack(cross, kept, teacher, student, after=()):
+    anywhere = pl.BlockSpec(memory_space=pl.ANY)
+    return pl.pallas_call(
+        functools.partial(pack_kernel, cross),
+        out_shape=[jax.ShapeDtypeStruct((MESSAGE, LANES), jnp.bfloat16)] * 16,
+        grid_spec=pltpu.PrefetchScalarGridSpec(
+            num_scalar_prefetch=1,
+            grid=(1,),
+            in_specs=[anywhere] * (2 + len(after)),
+            out_specs=[whole_block((MESSAGE, LANES))] * 16,
+            scratch_shapes=[
+                pltpu.VMEM((HEAD_SIZE, 2, ROWS, 2 * GROUP * TREL), jnp.bfloat16),
+                pltpu.VMEM((HEAD_SIZE, 5, 2, ROWS, HD), jnp.bfloat16),
+                pltpu.SemaphoreType.DMA((HEAD_SIZE, 6)),
+            ],
+        ),
+        name="pack_cross" if cross else "pack_near",
+    )(kept, teacher, student, *after)
+
+
+def whole_block(shape):
+    return pl.BlockSpec(shape, lambda *_: (0,) * len(shape), pipeline_mode=pl.Buffered(1))
+
+
+def nt_dot(a, b):
+    return lax.dot_general(a, b, (((1,), (1,)), ((), ())), preferred_element_type=jnp.float32)
+
+
+def shift_of(rows, width, factor):
+    norm = jnp.sqrt(nt_dot(jnp.ones((8, LANES), jnp.bfloat16), rows * rows))
+    return norm * (norm + LIMIT * math.sqrt(width)) * (0.5 * factor)
+
+
+def split_terms(row, scale):
+    scaled = row * scale
+    high = scaled.astype(jnp.bfloat16)
+    return high, (scaled - high.astype(jnp.float32)).astype(jnp.bfloat16)
+
+
+def prepared_shapes(blocks):
+    count = blocks * BLOCK
+    bf16 = jnp.bfloat16
+    return [
+        ((UNITS, count, LANES), bf16),
+        ((UNITS, count, LANES), bf16),
+        ((UNITS, count, 2 * LANES), bf16),
+        ((UNITS, count, 2 * LANES), bf16),
+        ((UNITS, 2, blocks, 8, BLOCK), jnp.float32),
+    ]
+
+
+def prepare(messages, made):
+    key_t, key_s, query_t, query_s, shifts = made
+    lane = lax.broadcasted_iota(jnp.int32, (ROWS, LANES), 1)
+    rel = (lane - CHUNK * (lax.axis_index("seq") & 3)) & (LANES - 1)
+    in_first = rel < SREL
+    in_tail = rel < CHUNK
+    zero = jnp.zeros((ROWS, LANES), jnp.float32)
+    for k, message in enumerate(messages):
+        start = (k // 4) * BLOCK + (lax.axis_index("head") ^ (k % 4)) * ROWS
+        at = pl.ds(pl.multiple_of(start, ROWS), ROWS)
+        tail = message[3 * LANES :, :].astype(jnp.float32)
+        for b in range(2):
+            main = message[2 * LANES + b * ROWS : 2 * LANES + (b + 1) * ROWS, :].astype(jnp.float32)
+            parts = [
+                pltpu.roll(tail, LANES - g * CHUNK, 1) if g else tail for g in (2 * b, 2 * b + 1)
+            ]
+            own = jnp.concatenate(parts, axis=0)
+            both = (jnp.where(in_first, main, zero), jnp.where(in_tail, own, jnp.where(in_first, zero, main)))
+            for w in range(2):
+                u = 2 * b + w
+                key = message[w * LANES + b * ROWS : w * LANES + (b + 1) * ROWS, :]
+                key_t[u, at, :] = key
+                query_t[u, at, 0:LANES], query_t[u, at, LANES:] = split_terms(key.astype(jnp.float32), SCALE_T)
+                key_s[u, at, :] = both[w].astype(jnp.bfloat16)
+                query_s[u, at, 0:LANES], query_s[u, at, LANES:] = split_terms(both[w], SCALE_S)
+
+    def shift(u, carry):
+        for block in range(len(messages) // 4):
+            rows = slice(block * BLOCK, (block + 1) * BLOCK)
+            shifts[u, 0, block] = shift_of(key_t[u, rows, :], TREL, SCALE_T)
+            shifts[u, 1, block] = shift_of(key_s[u, rows, :], SREL, SCALE_S)
+        return carry
+
+    lax.fori_loop(0, UNITS, shift, 0)
+
+
+def tile_sums(u, keys, key_block, queries, query_block, allowed=None):
+    rows = pl.ds(pl.multiple_of(key_block * BLOCK, BLOCK), BLOCK)
+    cols = pl.ds(pl.multiple_of(query_block * BLOCK, BLOCK), BLOCK)
+    tile = (BLOCK // 8, 8, BLOCK)
+    key_t, key_s = keys[0][u, rows, :], keys[1][u, rows, :]
+    x_t = nt_dot(jnp.concatenate([key_t, key_t], axis=1), queries[2][u, cols, :])
+    x_s = nt_dot(jnp.concatenate([key_s, key_s], axis=1), queries[3][u, cols, :])
+    x_t = x_t.reshape(tile) - queries[4][u, 0, query_block][None]
+    x_s = x_s.reshape(tile) - queries[4][u, 1, query_block][None]
+    w_t = jnp.exp2(x_t)
+    w_s = jnp.exp2(x_s)
+    if allowed is not None:
+        w_t = jnp.where(allowed, w_t, 0.0)
+        w_s = jnp.where(allowed, w_s, 0.0)
+    return jnp.sum(w_t, axis=0), jnp.sum(w_t * (x_t - x_s), axis=0), jnp.sum(w_s, axis=0)
+
+
+def causal_tile():
+    tile = (BLOCK // 8, 8, BLOCK)
+    key_in = lax.broadcasted_iota(jnp.int32, tile, 0) * 8 + lax.broadcasted_iota(jnp.int32, tile, 1)
+    return key_in <= lax.broadcasted_iota(jnp.int32, tile, 2)
+
+
+def over_units(tiles, body):
+    some = max(1, min(UNITS, 8 // tiles))
+
+    def step(i, carry):
+        for j in range(some):
+            body(i * some + j)
+        return carry
+
+    if some == UNITS:
+        step(0, 0)
+    else:
+        lax.fori_loop(0, UNITS // some, step, 0)
+
+
+def add_to(sums, slot, u, more):
+    for i in range(3):
+        sums[slot, u, i] += more[i]
+
+
+def pairs_inside(seq, base, blocks, made, sums):
+    allowed = causal_tile()
+
+    def unit(u):
+        for m in range(blocks):
+            for n in range(m + 1, blocks):
+                ahead = (seq ^ (base + m)) < (seq ^ (base + n))
+                key_block = jnp.where(ahead, m, n)
+                query_block = jnp.where(ahead, n, m)
+                add_to(sums, base + query_block, u, tile_sums(u, made, key_block, made, query_block))
+        for m in range(blocks):
+            add_to(sums, base + m, u, tile_sums(u, made, m, made, m, allowed))
+
+    over_units(blocks * (blocks + 1) // 2, unit)
+
+
+def pairs_between(seq, old_base, old_blocks, old, new_base, new_blocks, new, sums):
+    ahead = (seq ^ old_base) < (seq ^ new_base)
+
+    def old_keys(u):
+        for n in range(new_blocks):
+            parts = [tile_sums(u, old, m, new, n) for m in range(old_blocks)]
+            add_to(sums, new_base + n, u, [sum(part[i] for part in parts) for i in range(3)])
+
+    def new_keys(u):
+        for m in range(old_blocks):
+            parts = [tile_sums(u, new, n, old, m) for n in range(new_blocks)]
+            add_to(sums, old_base + m, u, [sum(part[i] for part in parts) for i in range(3)])
+
+    @pl.when(ahead)
+    def _():
+        over_units(old_blocks * new_blocks, old_keys)
+
+    @pl.when(jnp.logical_not(ahead))
+    def _():
+        over_units(old_blocks * new_blocks, new_keys)
+
+
+def stage_kernel(base, blocks, older, last, *refs):
+    messages, refs = refs[: 4 * blocks], refs[4 * blocks :]
+    sets = []
+    for start, size in older:
+        sets.append((start, size, refs[:5]))
+        refs = refs[5:]
+    before = None
+    if older:
+        before, refs = refs[0], refs[1:]
+    if last:
+        out_ref, made, sums = refs[0], refs[1:6], refs[6]
+    else:
+        made, sums = refs[:5], refs[5]
+    seq = lax.axis_index("seq")
+    sums[...] = jnp.zeros(sums.shape, jnp.float32) if before is None else before[...]
+    prepare(messages, made)
+    for start, size, old in sets:
+        pairs_between(seq, start, size, old, base, blocks, made, sums)
+    pairs_inside(seq, base, blocks, made, sums)
+    if last:
+        for m in range(SEQ_SIZE):
+            total = jnp.sum(sums[m], axis=2)
+            total_t, total_c, total_s = total[:, 0], total[:, 1], total[:, 2]
+            out_ref[seq ^ m] = (total_c / total_t - jnp.log2(total_t) + jnp.log2(total_s)) * LN2
+
+
+def stage(base, blocks, older, messages, old_sets, before, last=False):
+    made_shapes = prepared_shapes(blocks)
+    sums_shape = (SEQ_SIZE, UNITS, 3, 8, BLOCK)
+    out_shape = (SEQ_SIZE, UNITS, BLOCK)
+    if last:
+        outs, scratch = [(out_shape, jnp.float32)], made_shapes + [(sums_shape, jnp.float32)]
+    else:
+        outs, scratch = made_shapes + [(sums_shape, jnp.float32)], []
+    inputs = list(messages) + [array for old in old_sets for array in old] + ([before] if older else [])
+    return pl.pallas_call(
+        functools.partial(stage_kernel, base, blocks, older, last),
+        out_shape=[jax.ShapeDtypeStruct(shape, dtype) for shape, dtype in outs],
+        grid_spec=pl.GridSpec(
+            grid=(1,),
+            in_specs=[whole_block(array.shape) for array in inputs],
+            out_specs=[whole_block(shape) for shape, _ in outs],
+            scratch_shapes=[pltpu.VMEM(shape, dtype) for shape, dtype in scratch],
+        ),
+        compiler_params=pltpu.CompilerParams(vmem_limit_bytes=24 * 1024 * 1024),
+    )(*inputs)
+
+
+def packed_shards(teacher, student, kept):
+    batch = teacher.shape[0]
+
+    def exchange(message, k):
+        pairs = [(i, i ^ k) for i in range(SEQ_SIZE * HEAD_SIZE)]
+        return lax.ppermute(message, ("seq", "head"), pairs)
+
+    far = pack(1, kept, teacher, student)
+    got = {}
+    for k in range(16, 32):
+        got[k] = exchange(far[k - 16], k)
+    near = pack(0, kept, teacher, student, (far[15],))
+    got[0] = near[0]
+    for k in range(1, 16):
+        got[k] = exchange(near[k], k)
+    messages = [got[k] for k in range(32)]
+    older, sums = [], None
+    for base, blocks in STAGES:
+        *made, sums = stage(
+            base,
+            blocks,
+            tuple(entry[:2] for entry in older),
+            messages[4 * base : 4 * (base + blocks)],
+            [entry[2] for entry in older],
+            sums,
+            last=(base, blocks) == STAGES[-1],
+        )
+        older.append((base, blocks, made))
+    mine = sums
+    done = lax.all_to_all(mine, "seq", 0, 0, tiled=True)
+    pair = RELH // HEAD_SIZE // SEQ_SIZE
+    done = done.reshape(SEQ_SIZE, batch, pair, BLOCK)
+    return jnp.transpose(done, (1, 0, 2, 3)).reshape(batch, RELH // HEAD_SIZE, BLOCK)
 
 
 NEG_FILL = -1e30
@@ -67,7 +388,7 @@
 
 
 def batch_inside(local, head_count, width):
-    seq_count_b, rows, columns = local.shape
+    seq_count_b, rows, _ = local.shape
     folded = local.reshape(seq_count_b, rows, head_count, width)
     return jnp.transpose(folded, (1, 0, 2, 3)).reshape(rows, seq_count_b * head_count * width)
 
@@ -109,6 +430,22 @@
 
 def solution(mesh):
     placed = (P(None, ("seq", "head"), None), P(None, ("seq", "head"), None), P())
-    return jax.shard_map(
-        shards, mesh=mesh, in_specs=placed, out_specs=P(None, "head", "seq"), check_vma=False
-    )
+    sizes = dict(mesh.shape)
+
+    def run(teacher, student, kept):
+        batch, length = teacher.shape[0], teacher.shape[1]
+        fits = (
+            (sizes["seq"], sizes["head"]) == (SEQ_SIZE, HEAD_SIZE)
+            and batch == 2
+            and length == SEQ_SIZE * HEAD_SIZE * ROWS
+        )
+        step = jax.shard_map(
+            packed_shards if fits else shards,
+            mesh=mesh,
+            in_specs=placed,
+            out_specs=P(None, "head", "seq"),
+            check_vma=False,
+        )
+        return step(teacher, student, kept)
+
+    return run

time: 601 us -> 126 us (0.21)
  the two profiles are of different devices: /device:TPU:25 before, /device:TPU:0 now
where the time goes in v3:
time: 126 us; the launch traced here: 125 us
  starting transfers between devices  63.8 us (51%)
  Pallas kernels  30.9 us (25%)
  waiting for transfers between devices  18.1 us (14%)
  blocking collectives  10.9 us (9%)
  local copies, waits for them, and re-layouts  1.59 us (1%)
    ppermute x31, starting transfers between devices, exchange(): return lax.ppermute(message, ('seq', 'head'), pairs)  63.8 us
    pallas_call x5, Pallas kernels, stage(): pl.pallas_call(functools.partial(stage_kernel, base, blocks, older, last)...  23.5 us
    ppermute x31, waiting for transfers between devices, exchange(): return lax.ppermute(message, ('seq', 'head'), pairs)  18.1 us
    all_to_all x1, blocking collectives, packed_shards(): done = lax.all_to_all(mine, 'seq', 0, 0, tiled=True)  10.9 us
    pallas_call x2, Pallas kernels, pack(): pl.pallas_call(functools.partial(pack_kernel, cross), out_shape=[jax.Shap...  7.39 us
  transfers between devices with their start and end apart: 31, of which 8 were waited for; matrix products, arithmetic and copies ran while one was open for 0% of the time, Pallas kernels for 18%

profile of v3, /device:TPU:0, one launch (start us, length us, event | category | flops | bytes accessed | tf_op | source)
XLA Modules:
  0.0 125.5 jit_solution(6677492337312807358)
XLA Ops:
  0.0 3.7 %pack_cross.1 = (bf16[416,128]{1,0:T(8,128)(2,1)}, bf16[416,128]{1,0:T(8,128)(2,1)}, bf16[416,128]{1,0:T(8,128)(2,1)}, bf16[416,128]{1,0:T(8,128)(2,1)}, bf16[41...) custom-call(s32[40]{0:T(128)} %kept_ref.3, ...), custom_call_target="tpu_custom_call" | custom-call | tf_op jit(solution)/shard_map/pack_cross/pallas_call | solution.py:87
  3.7 4.1 %collective-permute-start.11 = (bf16[416,128]{1,0:T(8,128)(2,1)}, bf16[416,128]{1,0:T(8,128)(2,1)S(1)}, u32[]{:S(2)}, u32[]{:S(2)}) collective-permute-start(bf16[416,128]{1,0:T(8,128)(2,1)} %get-tuple-element.78), channel_id=1, source_target_pairs={{0,16},{1,17},{2,18},{3,19},{4,20},{5,21},{6,22},{7,23},{8,24},{9,... | collective-permute-start | bytes 319496 | tf_op jit(solution)/shard_map/ppermute | solution.py:305
  7.8 3.0 %collective-permute-start.13 = (bf16[416,128]{1,0:T(8,128)(2,1)}, bf16[416,128]{1,0:T(8,128)(2,1)S(1)}, u32[]{:S(2)}, u32[]{:S(2)}) collective-permute-start(bf16[416,128]{1,0:T(8,128)(2,1)} %get-tuple-element.80), channel_id=1, source_target_pairs={{0,18},{1,19},{2,16},{3,17},{4,22},{5,23},{6,20},{7,21},{8,26},{9,... | collective-permute-start | bytes 319496 | tf_op jit(solution)/shard_map/ppermute | solution.py:305
  11.4 3.5 %collective-permute-start.15 = (bf16[416,128]{1,0:T(8,128)(2,1)}, bf16[416,128]{1,0:T(8,128)(2,1)S(1)}, u32[]{:S(2)}, u32[]{:S(2)}) collective-permute-start(bf16[416,128]{1,0:T(8,128)(2,1)} %get-tuple-element.82), channel_id=1, source_target_pairs={{0,20},{1,21},{2,22},{3,23},{4,16},{5,17},{6,18},{7,19},{8,28},{9,... | collective-permute-start | bytes 319496 | tf_op jit(solution)/shard_map/ppermute | solution.py:305
  14.9 8.3 %collective-permute-done.11.refs_0_ = bf16[416,128]{1,0:T(8,128)(2,1)S(1)} collective-permute-done((bf16[416,128]{1,0:T(8,128)(2,1)}, bf16[416,128]{1,0:T(8,128)(2,1)S(1)}, u32[]{:S(2)}, u32[]{:S(2)}) %collective-permute-start.11) | collective-permute-done | bytes 106528 | tf_op jit(solution)/shard_map/ppermute | solution.py:305
  23.8 3.5 %collective-permute-start.17 = (bf16[416,128]{1,0:T(8,128)(2,1)}, bf16[416,128]{1,0:T(8,128)(2,1)S(1)}, u32[]{:S(2)}, u32[]{:S(2)}) collective-permute-start(bf16[416,128]{1,0:T(8,128)(2,1)} %get-tuple-element.84), channel_id=1, source_target_pairs={{0,22},{1,23},{2,20},{3,21},{4,18},{5,19},{6,16},{7,17},{8,30},{9,... | collective-permute-start | bytes 319496 | tf_op jit(solution)/shard_map/ppermute | solution.py:305
  27.4 4.0 %collective-permute-done.13.refs_2_ = bf16[416,128]{1,0:T(8,128)(2,1)S(1)} collective-permute-done((bf16[416,128]{1,0:T(8,128)(2,1)}, bf16[416,128]{1,0:T(8,128)(2,1)S(1)}, u32[]{:S(2)}, u32[]{:S(2)}) %collective-permute-start.13) | collective-permute-done | bytes 106528 | tf_op jit(solution)/shard_map/ppermute | solution.py:305
  31.4 9.1 %collective-permute-start.27 = (bf16[416,128]{1,0:T(8,128)(2,1)}, bf16[416,128]{1,0:T(8,128)(2,1)S(1)}, u32[]{:S(2)}, u32[]{:S(2)}) collective-permute-start(bf16[416,128]{1,0:T(8,128)(2,1)} %get-tuple-element.106), channel_id=1, source_target_pairs={{0,24},{1,25},{2,26},{3,27},{4,28},{5,29},{6,30},{7,31},{8,16},{9,... | collective-permute-start | bytes 319496 | tf_op jit(solution)/shard_map/ppermute | solution.py:305
  42.4 3.5 %collective-permute-start.29 = (bf16[416,128]{1,0:T(8,128)(2,1)}, bf16[416,128]{1,0:T(8,128)(2,1)S(1)}, u32[]{:S(2)}, u32[]{:S(2)}) collective-permute-start(bf16[416,128]{1,0:T(8,128)(2,1)} %get-tuple-element.108), channel_id=1, source_target_pairs={{0,26},{1,27},{2,24},{3,25},{4,30},{5,31},{6,28},{7,29},{8,18},{9,... | collective-permute-start | bytes 319496 | tf_op jit(solution)/shard_map/ppermute | solution.py:305
  46.0 3.7 %pack_near.1 = (bf16[416,128]{1,0:T(8,128)(2,1)}, bf16[416,128]{1,0:T(8,128)(2,1)}, bf16[416,128]{1,0:T(8,128)(2,1)}, bf16[416,128]{1,0:T(8,128)(2,1)}, bf16[416...) custom-call(s32[40]{0:T(128)} %kept_ref.3, ...), custom_call_target="tpu_custom_call" | custom-call | tf_op jit(solution)/shard_map/pack_near/pallas_call | solution.py:87
  49.7 3.8 %collective-permute-done.17.refs_6_ = bf16[416,128]{1,0:T(8,128)(2,1)S(1)} collective-permute-done((bf16[416,128]{1,0:T(8,128)(2,1)}, bf16[416,128]{1,0:T(8,128)(2,1)S(1)}, u32[]{:S(2)}, u32[]{:S(2)}) %collective-permute-start.17) | collective-permute-done | bytes 106528 | tf_op jit(solution)/shard_map/ppermute | solution.py:305
  53.6 3.3 %collective-permute-start.6 = (bf16[416,128]{1,0:T(8,128)(2,1)}, bf16[416,128]{1,0:T(8,128)(2,1)S(1)}, u32[]{:S(2)}, u32[]{:S(2)}) collective-permute-start(bf16[416,128]{1,0:T(8,128)(2,1)} %get-tuple-element.68), channel_id=1, source_target_pairs={{0,3},{1,2},{2,1},{3,0},{4,7},{5,6},{6,5},{7,4},{8,11},{9,10},{10,... | collective-permute-start | bytes 319496 | tf_op jit(solution)/shard_map/ppermute | solution.py:305
  58.8 2.6 %collective-permute-start.10 = (bf16[416,128]{1,0:T(8,128)(2,1)}, bf16[416,128]{1,0:T(8,128)(2,1)S(1)}, u32[]{:S(2)}, u32[]{:S(2)}) collective-permute-start(bf16[416,128]{1,0:T(8,128)(2,1)} %get-tuple-element.72), channel_id=1, source_target_pairs={{0,7},{1,6},{2,5},{3,4},{4,3},{5,2},{6,1},{7,0},{8,15},{9,14},{10,... | collective-permute-start | bytes 319496 | tf_op jit(solution)/shard_map/ppermute | solution.py:305
  62.0 3.2 %collective-permute-start.19 = (bf16[416,128]{1,0:T(8,128)(2,1)}, bf16[416,128]{1,0:T(8,128)(2,1)S(1)}, u32[]{:S(2)}, u32[]{:S(2)}) collective-permute-start(bf16[416,128]{1,0:T(8,128)(2,1)} %get-tuple-element.92), channel_id=1, source_target_pairs={{0,8},{1,9},{2,10},{3,11},{4,12},{5,13},{6,14},{7,15},{8,0},{9,1},... | collective-permute-start | bytes 319496 | tf_op jit(solution)/shard_map/ppermute | solution.py:305
  68.4 3.9 %collective-permute-start.23 = (bf16[416,128]{1,0:T(8,128)(2,1)}, bf16[416,128]{1,0:T(8,128)(2,1)S(1)}, u32[]{:S(2)}, u32[]{:S(2)}) collective-permute-start(bf16[416,128]{1,0:T(8,128)(2,1)} %get-tuple-element.96), channel_id=1, source_target_pairs={{0,12},{1,13},{2,14},{3,15},{4,8},{5,9},{6,10},{7,11},{8,4},{9,5},... | collective-permute-start | bytes 319496 | tf_op jit(solution)/shard_map/ppermute | solution.py:305
  75.6 3.9 %collective-permute-start.30 = (bf16[416,128]{1,0:T(8,128)(2,1)S(1)}, bf16[416,128]{1,0:T(8,128)(2,1)S(1)}, u32[]{:S(2)}, u32[]{:S(2)}) collective-permute-start(bf16[416,128]{1,0:T(8,128)(2,1)S(1)} %copy-done.5), channel_id=1, source_target_pairs={{0,27},{1,26},{2,25},{3,24},{4,31},{5,30},{6,29},{7,28},{8,19},{9,... | collective-permute-start | bytes 319496 | tf_op jit(solution)/shard_map/ppermute | solution.py:305
  79.5 2.3 %collective-permute-start = (bf16[416,128]{1,0:T(8,128)(2,1)S(1)}, bf16[416,128]{1,0:T(8,128)(2,1)S(1)}, u32[]{:S(2)}, u32[]{:S(2)}) collective-permute-start(bf16[416,128]{1,0:T(8,128)(2,1)S(1)} %copy-done.4), channel_id=1, source_target_pairs={{0,28},{1,29},{2,30},{3,31},{4,24},{5,25},{6,26},{7,27},{8,20},{9,... | collective-permute-start | bytes 319496 | tf_op jit(solution)/shard_map/ppermute | solution.py:305
  83.5 3.7 %collective-permute-start.2 = (bf16[416,128]{1,0:T(8,128)(2,1)S(1)}, bf16[416,128]{1,0:T(8,128)(2,1)S(1)}, u32[]{:S(2)}, u32[]{:S(2)}) collective-permute-start(bf16[416,128]{1,0:T(8,128)(2,1)S(1)} %copy-done.2), channel_id=1, source_target_pairs={{0,30},{1,31},{2,28},{3,29},{4,26},{5,27},{6,24},{7,25},{8,22},{9,... | collective-permute-start | bytes 319496 | tf_op jit(solution)/shard_map/ppermute | solution.py:305
  90.2 2.8 %shard_map.37 = (bf16[4,512,128]{2,1,0:T(8,128)(2,1)S(1)}, bf16[4,512,128]{2,1,0:T(8,128)(2,1)S(1)}, bf16[4,512,256]{2,1,0:T(8,128)(2,1)S(1)}, bf16[4,512,256]{2...) custom-call(bf16[416,128]{1,0:T(8,128)(2,1)S(1)} %copy-done, ...), custom_call_target="tpu_custom_call" | custom-call | tf_op jit(solution)/shard_map/pallas_call | solution.py:287
  93.1 4.7 %shard_map.38 = (bf16[4,512,128]{2,1,0:T(8,128)(2,1)S(1)}, bf16[4,512,128]{2,1,0:T(8,128)(2,1)S(1)}, bf16[4,512,256]{2,1,0:T(8,128)(2,1)S(1)}, bf16[4,512,256]{2...) custom-call(bf16[416,128]{1,0:T(8,128)(2,1)S(1)} %collective-permute-done.11.refs_0_, ...), custom_call_target="tpu_custom_call" | custom-call | tf_op jit(solution)/shard_map/pallas_call | solution.py:287
  97.8 6.6 %shard_map.39 = (bf16[4,512,128]{2,1,0:T(8,128)(2,1)S(1)}, bf16[4,512,128]{2,1,0:T(8,128)(2,1)S(1)}, bf16[4,512,256]{2,1,0:T(8,128)(2,1)S(1)}, bf16[4,512,256]{2...) custom-call(bf16[416,128]{1,0:T(8,128)(2,1)S(1)} %collective-permute-done.19.refs_0_, ...), custom_call_target="tpu_custom_call" | custom-call | tf_op jit(solution)/shard_map/pallas_call | solution.py:287
  104.4 4.2 %shard_map.40 = (bf16[4,256,128]{2,1,0:T(8,128)(2,1)S(1)}, bf16[4,256,128]{2,1,0:T(8,128)(2,1)S(1)}, bf16[4,256,256]{2,1,0:T(8,128)(2,1)S(1)}, bf16[4,256,256]{2...) custom-call(bf16[416,128]{1,0:T(8,128)(2,1)S(1)} %collective-permute-done.27.refs_0_, ...), custom_call_target="tpu_custom_call" | custom-call | tf_op jit(solution)/shard_map/pallas_call | solution.py:287
  108.7 5.2 %shard_map.41 = f32[8,4,256]{2,1,0:T(4,128)S(1)} custom-call(bf16[416,128]{1,0:T(8,128)(2,1)S(1)} %collective-permute-done.refs_0_, bf16[416,128]{1,0:T(8,128)(2,1)S(1)} %collective-permute-done.1.refs_1_, bf16[416,128]{1,0:T(8,128)(2,1)S(1)} %collective-permute-done.2.refs_2_, bf16[416,128]{1,0:T(8,128)(2,1)S(1)} %collective-permute-done.3.refs_3_, ...), custom_call_target="tpu_custom_call" | custom-call | tf_op jit(solution)/shard_map/pallas_call | solution.py:287
  113.9 10.9 %all_to_all.5 = f32[8,4,256]{2,1,0:T(4,128)S(1)} all-to-all(f32[8,4,256]{2,1,0:T(4,128)S(1)} %shard_map.41), channel_id=1, replica_groups=mesh['seq'=8,'head'=4] {'seq'}, dimensions={0} | all-to-all | bytes 65536 | tf_op jit(solution)/shard_map/all_to_all | solution.py:329
  (61 shorter events, 17.6 us)
Async XLA Ops:
  3.7 19.6 %collective-permute-start.11 = (bf16[416,128]{1,0:T(8,128)(2,1)}, bf16[416,128]{1,0:T(8,128)(2,1)S(1)}, u32[]{:S(2)}, u32[]{:S(2)}) collective-permute-start(bf16[416,128]{1,0:T(8,128)(2,1)} %get-tuple-element.78), channel_id=1, source_target_pairs={{0,16},{1,17},{2,18},{3,19},{4,20},{5,21},{6,22},{7,23},{8,24},{9,... | collective-permute-start | bytes 319496 | tf_op jit(solution)/shard_map/ppermute | solution.py:305
  7.8 16.0 %collective-permute-start.12 = (bf16[416,128]{1,0:T(8,128)(2,1)}, bf16[416,128]{1,0:T(8,128)(2,1)S(1)}, u32[]{:S(2)}, u32[]{:S(2)}) collective-permute-start(bf16[416,128]{1,0:T(8,128)(2,1)} %get-tuple-element.79), channel_id=1, source_target_pairs={{0,17},{1,16},{2,19},{3,18},{4,21},{5,20},{6,23},{7,22},{8,25},{9,... | collective-permute-start | bytes 319496 | tf_op jit(solution)/shard_map/ppermute | solution.py:305
  7.8 23.5 %collective-permute-start.13 = (bf16[416,128]{1,0:T(8,128)(2,1)}, bf16[416,128]{1,0:T(8,128)(2,1)S(1)}, u32[]{:S(2)}, u32[]{:S(2)}) collective-permute-start(bf16[416,128]{1,0:T(8,128)(2,1)} %get-tuple-element.80), channel_id=1, source_target_pairs={{0,18},{1,19},{2,16},{3,17},{4,22},{5,23},{6,20},{7,21},{8,26},{9,... | collective-permute-start | bytes 319496 | tf_op jit(solution)/shard_map/ppermute | solution.py:305
  10.8 20.6 %collective-permute-start.14 = (bf16[416,128]{1,0:T(8,128)(2,1)}, bf16[416,128]{1,0:T(8,128)(2,1)S(1)}, u32[]{:S(2)}, u32[]{:S(2)}) collective-permute-start(bf16[416,128]{1,0:T(8,128)(2,1)} %get-tuple-element.81), channel_id=1, source_target_pairs={{0,19},{1,18},{2,17},{3,16},{4,23},{5,22},{6,21},{7,20},{8,27},{9,... | collective-permute-start | bytes 319496 | tf_op jit(solution)/shard_map/ppermute | solution.py:305
  11.4 29.1 %collective-permute-start.15 = (bf16[416,128]{1,0:T(8,128)(2,1)}, bf16[416,128]{1,0:T(8,128)(2,1)S(1)}, u32[]{:S(2)}, u32[]{:S(2)}) collective-permute-start(bf16[416,128]{1,0:T(8,128)(2,1)} %get-tuple-element.82), channel_id=1, source_target_pairs={{0,20},{1,21},{2,22},{3,23},{4,16},{5,17},{6,18},{7,19},{8,28},{9,... | collective-permute-start | bytes 319496 | tf_op jit(solution)/shard_map/ppermute | solution.py:305
  23.2 19.2 %collective-permute-start.16 = (bf16[416,128]{1,0:T(8,128)(2,1)}, bf16[416,128]{1,0:T(8,128)(2,1)S(1)}, u32[]{:S(2)}, u32[]{:S(2)}) collective-permute-start(bf16[416,128]{1,0:T(8,128)(2,1)} %get-tuple-element.83), channel_id=1, source_target_pairs={{0,21},{1,20},{2,23},{3,22},{4,17},{5,16},{6,19},{7,18},{8,29},{9,... | collective-permute-start | bytes 319496 | tf_op jit(solution)/shard_map/ppermute | solution.py:305
  23.8 29.7 %collective-permute-start.17 = (bf16[416,128]{1,0:T(8,128)(2,1)}, bf16[416,128]{1,0:T(8,128)(2,1)S(1)}, u32[]{:S(2)}, u32[]{:S(2)}) collective-permute-start(bf16[416,128]{1,0:T(8,128)(2,1)} %get-tuple-element.84), channel_id=1, source_target_pairs={{0,22},{1,23},{2,20},{3,21},{4,18},{5,19},{6,16},{7,17},{8,30},{9,... | collective-permute-start | bytes 319496 | tf_op jit(solution)/shard_map/ppermute | solution.py:305
  31.3 22.3 %collective-permute-start.18 = (bf16[416,128]{1,0:T(8,128)(2,1)}, bf16[416,128]{1,0:T(8,128)(2,1)S(1)}, u32[]{:S(2)}, u32[]{:S(2)}) collective-permute-start(bf16[416,128]{1,0:T(8,128)(2,1)} %get-tuple-element.85), channel_id=1, source_target_pairs={{0,23},{1,22},{2,21},{3,20},{4,19},{5,18},{6,17},{7,16},{8,31},{9,... | collective-permute-start | bytes 319496 | tf_op jit(solution)/shard_map/ppermute | solution.py:305
  31.4 22.2 %collective-permute-start.27 = (bf16[416,128]{1,0:T(8,128)(2,1)}, bf16[416,128]{1,0:T(8,128)(2,1)S(1)}, u32[]{:S(2)}, u32[]{:S(2)}) collective-permute-start(bf16[416,128]{1,0:T(8,128)(2,1)} %get-tuple-element.106), channel_id=1, source_target_pairs={{0,24},{1,25},{2,26},{3,27},{4,28},{5,29},{6,30},{7,31},{8,16},{9,... | collective-permute-start | bytes 319496 | tf_op jit(solution)/shard_map/ppermute | solution.py:305
  40.5 16.5 %collective-permute-start.28 = (bf16[416,128]{1,0:T(8,128)(2,1)}, bf16[416,128]{1,0:T(8,128)(2,1)S(1)}, u32[]{:S(2)}, u32[]{:S(2)}) collective-permute-start(bf16[416,128]{1,0:T(8,128)(2,1)} %get-tuple-element.107), channel_id=1, source_target_pairs={{0,25},{1,24},{2,27},{3,26},{4,29},{5,28},{6,31},{7,30},{8,17},{9,... | collective-permute-start | bytes 319496 | tf_op jit(solution)/shard_map/ppermute | solution.py:305
  42.4 14.5 %collective-permute-start.29 = (bf16[416,128]{1,0:T(8,128)(2,1)}, bf16[416,128]{1,0:T(8,128)(2,1)S(1)}, u32[]{:S(2)}, u32[]{:S(2)}) collective-permute-start(bf16[416,128]{1,0:T(8,128)(2,1)} %get-tuple-element.108), channel_id=1, source_target_pairs={{0,26},{1,27},{2,24},{3,25},{4,30},{5,31},{6,28},{7,29},{8,18},{9,... | collective-permute-start | bytes 319496 | tf_op jit(solution)/shard_map/ppermute | solution.py:305
  57.1 10.2 %collective-permute-start.9 = (bf16[416,128]{1,0:T(8,128)(2,1)}, bf16[416,128]{1,0:T(8,128)(2,1)S(1)}, u32[]{:S(2)}, u32[]{:S(2)}) collective-permute-start(bf16[416,128]{1,0:T(8,128)(2,1)} %get-tuple-element.71), channel_id=1, source_target_pairs={{0,6},{1,7},{2,4},{3,5},{4,2},{5,3},{6,0},{7,1},{8,14},{9,15},{10,... | collective-permute-start | bytes 319496 | tf_op jit(solution)/shard_map/ppermute | solution.py:305
  58.8 9.6 %collective-permute-start.10 = (bf16[416,128]{1,0:T(8,128)(2,1)}, bf16[416,128]{1,0:T(8,128)(2,1)S(1)}, u32[]{:S(2)}, u32[]{:S(2)}) collective-permute-start(bf16[416,128]{1,0:T(8,128)(2,1)} %get-tuple-element.72), channel_id=1, source_target_pairs={{0,7},{1,6},{2,5},{3,4},{4,3},{5,2},{6,1},{7,0},{8,15},{9,14},{10,... | collective-permute-start | bytes 319496 | tf_op jit(solution)/shard_map/ppermute | solution.py:305
  62.0 10.4 %collective-permute-start.19 = (bf16[416,128]{1,0:T(8,128)(2,1)}, bf16[416,128]{1,0:T(8,128)(2,1)S(1)}, u32[]{:S(2)}, u32[]{:S(2)}) collective-permute-start(bf16[416,128]{1,0:T(8,128)(2,1)} %get-tuple-element.92), channel_id=1, source_target_pairs={{0,8},{1,9},{2,10},{3,11},{4,12},{5,13},{6,14},{7,15},{8,0},{9,1},... | collective-permute-start | bytes 319496 | tf_op jit(solution)/shard_map/ppermute | solution.py:305
  65.1 9.1 %collective-permute-start.21 = (bf16[416,128]{1,0:T(8,128)(2,1)}, bf16[416,128]{1,0:T(8,128)(2,1)S(1)}, u32[]{:S(2)}, u32[]{:S(2)}) collective-permute-start(bf16[416,128]{1,0:T(8,128)(2,1)} %get-tuple-element.94), channel_id=1, source_target_pairs={{0,10},{1,11},{2,8},{3,9},{4,14},{5,15},{6,12},{7,13},{8,2},{9,3},... | collective-permute-start | bytes 319496 | tf_op jit(solution)/shard_map/ppermute | solution.py:305
  68.4 11.1 %collective-permute-start.23 = (bf16[416,128]{1,0:T(8,128)(2,1)}, bf16[416,128]{1,0:T(8,128)(2,1)S(1)}, u32[]{:S(2)}, u32[]{:S(2)}) collective-permute-start(bf16[416,128]{1,0:T(8,128)(2,1)} %get-tuple-element.96), channel_id=1, source_target_pairs={{0,12},{1,13},{2,14},{3,15},{4,8},{5,9},{6,10},{7,11},{8,4},{9,5},... | collective-permute-start | bytes 319496 | tf_op jit(solution)/shard_map/ppermute | solution.py:305
  72.3 9.5 %collective-permute-start.24 = (bf16[416,128]{1,0:T(8,128)(2,1)}, bf16[416,128]{1,0:T(8,128)(2,1)S(1)}, u32[]{:S(2)}, u32[]{:S(2)}) collective-permute-start(bf16[416,128]{1,0:T(8,128)(2,1)} %get-tuple-element.97), channel_id=1, source_target_pairs={{0,13},{1,12},{2,15},{3,14},{4,9},{5,8},{6,11},{7,10},{8,5},{9,4},... | collective-permute-start | bytes 319496 | tf_op jit(solution)/shard_map/ppermute | solution.py:305
  72.3 11.2 %collective-permute-start.25 = (bf16[416,128]{1,0:T(8,128)(2,1)}, bf16[416,128]{1,0:T(8,128)(2,1)S(1)}, u32[]{:S(2)}, u32[]{:S(2)}) collective-permute-start(bf16[416,128]{1,0:T(8,128)(2,1)} %get-tuple-element.98), channel_id=1, source_target_pairs={{0,14},{1,15},{2,12},{3,13},{4,10},{5,11},{6,8},{7,9},{8,6},{9,7},... | collective-permute-start | bytes 319496 | tf_op jit(solution)/shard_map/ppermute | solution.py:305
  74.2 13.1 %collective-permute-start.26 = (bf16[416,128]{1,0:T(8,128)(2,1)}, bf16[416,128]{1,0:T(8,128)(2,1)S(1)}, u32[]{:S(2)}, u32[]{:S(2)}) collective-permute-start(bf16[416,128]{1,0:T(8,128)(2,1)} %get-tuple-element.99), channel_id=1, source_target_pairs={{0,15},{1,14},{2,13},{3,12},{4,11},{5,10},{6,9},{7,8},{8,7},{9,6},... | collective-permute-start | bytes 319496 | tf_op jit(solution)/shard_map/ppermute | solution.py:305
  75.6 28.8 %collective-permute-start.30 = (bf16[416,128]{1,0:T(8,128)(2,1)S(1)}, bf16[416,128]{1,0:T(8,128)(2,1)S(1)}, u32[]{:S(2)}, u32[]{:S(2)}) collective-permute-start(bf16[416,128]{1,0:T(8,128)(2,1)S(1)} %copy-done.5), channel_id=1, source_target_pairs={{0,27},{1,26},{2,25},{3,24},{4,31},{5,30},{6,29},{7,28},{8,19},{9,... | collective-permute-start | bytes 319496 | tf_op jit(solution)/shard_map/ppermute | solution.py:305
  79.5 29.1 %collective-permute-start = (bf16[416,128]{1,0:T(8,128)(2,1)S(1)}, bf16[416,128]{1,0:T(8,128)(2,1)S(1)}, u32[]{:S(2)}, u32[]{:S(2)}) collective-permute-start(bf16[416,128]{1,0:T(8,128)(2,1)S(1)} %copy-done.4), channel_id=1, source_target_pairs={{0,28},{1,29},{2,30},{3,31},{4,24},{5,25},{6,26},{7,27},{8,20},{9,... | collective-permute-start | bytes 319496 | tf_op jit(solution)/shard_map/ppermute | solution.py:305
  81.8 26.8 %collective-permute-start.1 = (bf16[416,128]{1,0:T(8,128)(2,1)S(1)}, bf16[416,128]{1,0:T(8,128)(2,1)S(1)}, u32[]{:S(2)}, u32[]{:S(2)}) collective-permute-start(bf16[416,128]{1,0:T(8,128)(2,1)S(1)} %copy-done.3), channel_id=1, source_target_pairs={{0,29},{1,28},{2,31},{3,30},{4,25},{5,24},{6,27},{7,26},{8,21},{9,... | collective-permute-start | bytes 319496 | tf_op jit(solution)/shard_map/ppermute | solution.py:305
  83.5 25.1 %collective-permute-start.2 = (bf16[416,128]{1,0:T(8,128)(2,1)S(1)}, bf16[416,128]{1,0:T(8,128)(2,1)S(1)}, u32[]{:S(2)}, u32[]{:S(2)}) collective-permute-start(bf16[416,128]{1,0:T(8,128)(2,1)S(1)} %copy-done.2), channel_id=1, source_target_pairs={{0,30},{1,31},{2,28},{3,29},{4,26},{5,27},{6,24},{7,25},{8,22},{9,... | collective-permute-start | bytes 319496 | tf_op jit(solution)/shard_map/ppermute | solution.py:305
  87.3 21.4 %collective-permute-start.3 = (bf16[416,128]{1,0:T(8,128)(2,1)S(1)}, bf16[416,128]{1,0:T(8,128)(2,1)S(1)}, u32[]{:S(2)}, u32[]{:S(2)}) collective-permute-start(bf16[416,128]{1,0:T(8,128)(2,1)S(1)} %copy-done.1), channel_id=1, source_target_pairs={{0,31},{1,30},{2,29},{3,28},{4,27},{5,26},{6,25},{7,24},{8,23},{9,... | collective-permute-start | bytes 319496 | tf_op jit(solution)/shard_map/ppermute | solution.py:305
  (13 other events, 227.8 us)
